TPU v7x, 256 devices: a whole 4x4x8 slice. The times are simulated.
256 devices in a mesh: span: 16 (over y_lo, z), chord: 4 (over x), normal: 4 (over y_hi, core).
Axes of the slice: x: 4, y: 4 (y_hi: 2, y_lo: 2; y = y_hi * 2 + y_lo), z: 8, core: 2. Of those that a mesh axis runs over, the one named last changes fastest.
Arguments:
- adjoint: float32 [5, 128, 32, 512], P(None, 'span', 'chord', 'normal'), may hold values from -6 to 6
- jacobian: bfloat16 [7, 5, 5, 128, 32, 512], P(None, None, None, 'span', 'chord', 'normal'), may hold values from -1 to 1
- wall_table: float32 [3, 5, 5], replicated, may hold values from -3 to 3
- face_type: int32 [128, 32], P('span', 'chord'), may hold values from 0 to 2
- mesh_map: float32 [3, 5], replicated, may hold values from -2.5 to 2.5
- stiffness: float32 [7, 128, 32, 512], P(None, 'span', 'chord', 'normal'), may hold values from 0.1 to 1
- box_map: int32 [16, 4, 4], P('span', 'chord', 'normal'), may hold values from 0 to 15
- offsets: int32 [16, 4, 4, 3], P('span', 'chord', 'normal'), may hold values from 0 to 88, as said below
Outputs:
- mesh_adjoint: float32 [3, 128, 32, 512], P(None, 'span', 'chord', 'normal')
- ffd_grad: float32 [16, 3, 49152], P('span', None, ('chord', 'normal'))
Inputs may be any that keep to these rules, and one draw needn't show every extreme that they name: `offsets`: column 0 is at most 88, column 1 at most 24, column 2 at most 8, so every window lies inside its box.
All inputs are finite; a program needn't handle non-finite values.
Results may differ from a plain program's by a relative error of at most 0.0003.
Values sent between devices are 32-bit elements; how exact they have to be, the bound alone decides.
No kernel may reach another device: no remote copies, remote signals or barrier semaphores. Data moves between devices by JAX's collectives and lax.ppermute only.
A program may use at most 192 MiB of HBM per device.

v0:
```python
import math

import jax
import jax.numpy as jnp
import numpy as np
from jax import lax
from jax.sharding import PartitionSpec as P

LA = 96
LB = 32
LC = 16
WA = 8
WB = 8
WC = 8
LAT = 49152


HIGHEST = lax.Precision.HIGHEST


def padded_2(shard, sides, width):
    for axis, dim in sides:
        count, length = (lax.axis_size(axis), shard.shape[dim])
        up = [(i, (i + 1) % count) for i in range(count - 1)]
        down = [(j, i) for i, j in up]
        last = lax.slice_in_dim(shard, length - width, length, axis=dim)
        first = lax.slice_in_dim(shard, 0, width, axis=dim)
        before = lax.ppermute(last, axis, up)
        after = lax.ppermute(first, axis, down)
        shard = jnp.concatenate([before, shard, after], axis=dim)
    return shard


def neighbours(padded):
    width_x = padded.shape[1] - 2
    width_y = padded.shape[2] - 2
    width_z = padded.shape[3] - 2

    def cut(step_x, step_y, step_z):
        return padded[
            :,
            1 + step_x : 1 + step_x + width_x,
            1 + step_y : 1 + step_y + width_y,
            1 + step_z : 1 + step_z + width_z,
        ]

    return [
        cut(0, 0, 0),
        cut(-1, 0, 0),
        cut(1, 0, 0),
        cut(0, -1, 0),
        cut(0, 1, 0),
        cut(0, 0, -1),
        cut(0, 0, 1),
    ]


def flux_sweep(shifted, jacobian):
    total = jnp.zeros(jacobian.shape[2:], jnp.float32)
    for direction in range(7):
        for source in range(5):
            total = (
                total
                + jacobian[direction, source].astype(jnp.float32) * shifted[direction][source][None]
            )
    return total


def wall_term(adjoint_layer, face_type, wall_table):
    onehot = (face_type[None] == jnp.arange(3, dtype=jnp.int32)[:, None, None]).astype(jnp.float32)
    table = jnp.einsum("tpq,txy->pqxy", wall_table, onehot, precision=HIGHEST)
    return jnp.einsum("pqxy,pxy->qxy", table, adjoint_layer, precision=HIGHEST)


def elastic_apply(shifted, stiffness, diagonal):
    total = diagonal[None] * shifted[0]
    for direction in range(1, 7):
        total = total - stiffness[direction][None] * shifted[direction]
    return total


def bernstein(count, cells):
    degree = count - 1
    binomial = jnp.asarray(
        np.array([math.comb(degree, point) for point in range(count)]), dtype=jnp.float32
    )
    coords = (jnp.arange(cells, dtype=jnp.float32) + 0.5) / cells
    powers = jnp.arange(count, dtype=jnp.float32)
    return (
        binomial[:, None]
        * coords[None, :] ** powers[:, None]
        * (1.0 - coords[None, :]) ** (degree - powers)[:, None]
    )


def ffd_window(field):
    along_x = bernstein(WA, field.shape[1])
    along_y = bernstein(WB, field.shape[2])
    along_z = bernstein(WC, field.shape[3])
    inner = jnp.einsum("cxyz,gz->cxyg", field, along_z, precision=HIGHEST)
    inner = jnp.einsum("cxyg,by->cxbg", inner, along_y, precision=HIGHEST)
    return 8.0 * jnp.einsum("cxbg,ax->cabg", inner, along_x, precision=HIGHEST)


def mesh_halo(field):
    return padded_2(field, (("span", 1), ("chord", 2), ("normal", 3)), 1)


def local(adjoint, jacobian, wall_table, face_type, mesh_map, stiffness, box_map, offsets):
    padded = padded_2(adjoint, (("span", 1), ("chord", 2), ("normal", 3)), 1)
    residual = flux_sweep(neighbours(padded), jacobian)
    wall_on = (lax.axis_index("normal") == 0).astype(jnp.float32)
    residual = residual.at[:, :, :, 0].add(
        wall_on * wall_term(adjoint[:, :, :, 0], face_type, wall_table)
    )
    sensitivity = jnp.einsum("rq,qxyz->rxyz", mesh_map, residual, precision=HIGHEST)
    diagonal = stiffness[0] + jnp.sum(stiffness[1:], axis=0)
    iterate = sensitivity / diagonal[None]
    for sweep in range(2):
        applied = elastic_apply(neighbours(mesh_halo(iterate)), stiffness, diagonal)
        iterate = iterate + (sensitivity - applied) / diagonal[None]
    window = ffd_window(iterate)
    groups = lax.axis_size(("chord", "normal"))
    share = LAT // groups
    zero = jnp.zeros((), jnp.int32)
    box_id = box_map[0, 0, 0]
    corner = offsets[0, 0, 0]
    boxes = lax.axis_size("span")
    full = jnp.zeros((boxes, 3, LA, LB, LC), jnp.float32)
    full = lax.dynamic_update_slice(
        full, window[None], (box_id, zero, corner[0], corner[1], corner[2])
    )
    full = (
        full.reshape(boxes, 3, groups, share)
        .transpose(0, 2, 1, 3)
        .reshape(boxes * groups, 3, share)
    )
    ffd_grad = lax.psum_scatter(full, ("span", "chord", "normal"), scatter_dimension=0, tiled=True)
    return (iterate, ffd_grad)


def solution(mesh):
    placed = (
        P(None, "span", "chord", "normal"),
        P(None, None, None, "span", "chord", "normal"),
        P(),
        P("span", "chord"),
        P(),
        P(None, "span", "chord", "normal"),
        P("span", "chord", "normal"),
        P("span", "chord", "normal", None),
    )
    return jax.shard_map(
        local,
        mesh=mesh,
        in_specs=placed,
        out_specs=(P(None, "span", "chord", "normal"), P("span", None, ("chord", "normal"))),
        check_vma=False,
    )
```

profile of v0, /device:TPU:1, one launch (start us, length us, event | category | flops | bytes accessed | tf_op | source)
XLA Modules:
  0.0 610.5 jit_solution(12975443884577358037)
XLA Ops:
  8.6 4.9 collective-permute-start
  20.8 1.6 copy.166
  22.5 1.7 copy.196
  24.1 1.7 copy.198
  25.8 1.6 copy.200
  27.5 1.6 copy.202
  29.1 1.6 copy.204
  30.7 1.6 copy.206
  32.3 1.6 copy.208
  35.6 1.6 copy.212
  38.8 1.7 copy.216
  43.7 1.7 copy.222
  45.4 1.7 copy.224
  47.1 1.6 copy.226
  48.8 1.7 copy.228
  50.5 1.6 copy.230
  53.7 1.7 copy.170
  55.3 1.6 copy.172
  58.6 1.8 copy.176
  62.0 1.6 copy.180
  65.2 1.6 copy.184
  66.8 1.6 copy.186
  70.1 1.7 copy.190
  71.8 1.6 copy.192
  76.6 1.7 copy.234
  85.6 4.0 collective-permute-start.2
  99.9 6.2 %collective-permute-start.4 = (f32[5,10,10,1]{3,2,1,0:T(8,128)S(1)}, f32[5,10,10,1]{3,2,1,0:T(8,128)S(1)}, u32[]{:S(2)}, u32[]{:S(2)}) collective-permute-start(f32[5,10,10,1]{3,2,1,0:T(8,128)S(1)} %get-tuple-element.65), channel_id=1, source_target_pairs={{0,1},{1,2},{2,3},{4,5},{5,6},{6,7},{8,9},{9,10},{10,11},{12,13},{... | collective-permute-start | bytes 6008 | tf_op jit(solution)/shard_map/ppermute | solution.py:28
  106.2 2.1 collective-permute-start.5
  111.3 5.6 collective-permute-done.5
  134.5 25.7 %fusion = f32[5,8,8,128]{2,1,0,3:T(8,128)S(1)} fusion(bf16[1,1,5,8,8,128]{4,3,2,5,1,0:T(8,128)(2,1)} %copy.234, bf16[1,1,5,8,8,128]{4,3,2,5,1,0:T(8,128)(2,1)} %copy.232, bf16[1,1,5,8,8,128]{4,3,2,5,1,0:T(8,128)(2,1)} %copy.230, bf16[1,1,5,8,8,128]{4,3,2,5,1,0:T(8,128)(2,1)} %copy.228, bf16[1,1,5,8,8,128]{4,3,2,5,1,0:T(8,128)(2,1)} %copy.226, ...), kind=kLoop, calls=%fused_computation.1 | loop fusion | flops 4259840 | bytes 4177920 | tf_op jit(solution)/shard_map/add | solution.py:63
  161.9 4.3 collective-permute-start.6
  167.5 3.2 collective-permute-done.7
  170.7 3.1 collective-permute-start.8
  175.8 2.6 collective-permute-done.9
  178.6 4.6 collective-permute-start.10
  183.2 1.9 collective-permute-start.11
  185.9 5.9 collective-permute-done.11
  192.1 4.0 collective-permute-start.12
  197.5 4.7 collective-permute-done.13
  202.1 3.1 collective-permute-start.14
  207.2 2.6 collective-permute-done.15
  210.0 4.3 collective-permute-start.16
  214.4 2.2 collective-permute-start.17
  224.5 23.8 %broadcast_in_dim.4 = f32[16,3,96,32,16]{4,3,2,1,0:T(8,128)} broadcast(f32[]{:T(128)} %constant.49.clone.1), dimensions={} | broadcast | bytes 9437188 | tf_op jit(solution)/shard_map/broadcast_in_dim | solution.py:129
  248.3 8.0 %dynamic_update_slice.3 = f32[16,3,96,32,16]{4,3,2,1,0:T(8,128)} dynamic-update-slice(f32[16,3,96,32,16]{4,3,2,1,0:T(8,128)} %broadcast_in_dim.4, f32[1,3,8,8,8]{4,3,2,1,0:T(8,128)S(1)} %copy.240, s32[]{:T(128)S(6)} %select_n.12, s32[]{:T(128)} %constant.48.clone.1, s32[]{:T(128)S(6)} %select_n.13, s32[]{:T(128)S(6)} %select_n.14, s32[]{:T(128)S(6)} %select_n.15) | dynamic-update-slice | bytes 12292 | tf_op jit(solution)/shard_map/dynamic_update_slice | solution.py:130
  256.4 60.3 %reshape.152 = f32[16,3,16,3072]{3,2,1,0:T(8,128)} reshape(f32[16,3,96,32,16]{4,3,2,1,0:T(8,128)} %dynamic_update_slice.3) | data formatting | bytes 18874368 | tf_op jit(solution)/shard_map/reshape | solution.py:134
  316.7 8.5 %copy.241 = f32[16,16,3,3072]{3,1,0,2:T(8,128)} copy(f32[16,16,3,3072]{3,1,2,0:T(8,128)} %bitcast.259) | data formatting | bytes 18874368 | tf_op jit(solution)/shard_map/transpose | solution.py:135
  325.2 276.9 %all-reduce.3.cloned.1.call-done = f32[256,3,3072]{2,0,1:T(8,128)} async-done(((f32[256,3,3072]{2,0,1:T(8,128)}), f32[256,3,3072]{2,0,1:T(8,128)}) %all-reduce.3.cloned.1.call-update) | async-done | bytes 9437200
  (138 shorter events, 77.3 us)
Async XLA Ops:
  7.2 12.6 %copy-start = (f32[3,5,5]{2,0,1:T(4,128)S(1)}, f32[3,5,5]{2,0,1:T(4,128)}, u32[]{:S(2)}) copy-start(f32[3,5,5]{2,0,1:T(4,128)} %param.15) | copy-start | bytes 904
  7.2 594.9 %all-reduce.3.cloned.1.call-start = ((), (), s32[]{:S(2)}) async-start(), calls=%async_computation | async-start | bytes 18874368
  8.6 74.1 %collective-permute-start = (f32[5,1,8,128]{3,2,1,0:T(8,128)}, f32[5,1,8,128]{3,2,1,0:T(8,128)}, u32[]{:S(2)}, u32[]{:S(2)}) collective-permute-start(f32[5,1,8,128]{3,2,1,0:T(8,128)} %get-tuple-element.115), channel_id=1, source_target_pairs={{0,16},{16,32},{32,48},{48,64},{64,80},{80,96},{96,112},{112,128},... | collective-permute-start | bytes 61448 | tf_op jit(solution)/shard_map/ppermute | solution.py:28
  13.5 4.5 copy-start.2
  13.5 6.2 %copy-start.3 = (f32[7,8,8,128]{3,2,1,0:T(8,128)S(1)}, f32[7,8,8,128]{3,2,1,0:T(8,128)}, u32[]{:S(2)}) copy-start(f32[7,8,8,128]{3,2,1,0:T(8,128)} %param.18) | copy-start | bytes 688132
  13.5 69.9 %collective-permute-start.1 = (f32[5,1,8,128]{3,2,1,0:T(8,128)}, f32[5,1,8,128]{3,2,1,0:T(8,128)}, u32[]{:S(2)}, u32[]{:S(2)}) collective-permute-start(f32[5,1,8,128]{3,2,1,0:T(8,128)} %get-tuple-element.114), channel_id=1, source_target_pairs={{16,0},{32,16},{48,32},{64,48},{80,64},{96,80},{112,96},{128,112},... | collective-permute-start | bytes 61448 | tf_op jit(solution)/shard_map/ppermute | solution.py:29
  16.5 3.2 copy-start.11
  71.8 6.5 %copy-start.8 = (f32[8,8,128]{2,1,0:T(8,128)S(1)}, f32[8,8,128]{2,1,0:T(8,128)}, u32[]{:S(2)}) copy-start(f32[8,8,128]{2,1,0:T(8,128)} %get-tuple-element.106) | copy-start | bytes 98308
  73.4 5.1 copy-start.7
  73.4 6.1 %copy-start.6 = (f32[8,8,128]{2,1,0:T(8,128)S(1)}, f32[8,8,128]{2,1,0:T(8,128)}, u32[]{:S(2)}) copy-start(f32[8,8,128]{2,1,0:T(8,128)} %get-tuple-element.109) | copy-start | bytes 98308
  73.4 7.1 %copy-start.5 = (f32[8,8,128]{2,1,0:T(8,128)S(1)}, f32[8,8,128]{2,1,0:T(8,128)}, u32[]{:S(2)}) copy-start(f32[8,8,128]{2,1,0:T(8,128)} %get-tuple-element.108) | copy-start | bytes 98308
  84.3 15.4 %collective-permute-start.3 = (f32[5,10,1,128]{3,2,1,0:T(1,128)S(1)}, f32[5,10,1,128]{3,2,1,0:T(1,128)S(1)}, u32[]{:S(2)}, u32[]{:S(2)}) collective-permute-start(f32[5,10,1,128]{3,2,1,0:T(1,128)S(1)} %get-tuple-element.91), channel_id=1, source_target_pairs={{4,0},{8,4},{12,8},{5,1},{9,5},{13,9},{6,2},{10,6},{14,10},{7,3},{... | collective-permute-start | bytes 76808 | tf_op jit(solution)/shard_map/ppermute | solution.py:29
  85.6 14.1 %collective-permute-start.2 = (f32[5,10,1,128]{3,2,1,0:T(1,128)S(1)}, f32[5,10,1,128]{3,2,1,0:T(1,128)S(1)}, u32[]{:S(2)}, u32[]{:S(2)}) collective-permute-start(f32[5,10,1,128]{3,2,1,0:T(1,128)S(1)} %get-tuple-element.90), channel_id=1, source_target_pairs={{0,4},{4,8},{8,12},{1,5},{5,9},{9,13},{2,6},{6,10},{10,14},{3,7},{... | collective-permute-start | bytes 76808 | tf_op jit(solution)/shard_map/ppermute | solution.py:28
  99.9 11.4 %collective-permute-start.4 = (f32[5,10,10,1]{3,2,1,0:T(8,128)S(1)}, f32[5,10,10,1]{3,2,1,0:T(8,128)S(1)}, u32[]{:S(2)}, u32[]{:S(2)}) collective-permute-start(f32[5,10,10,1]{3,2,1,0:T(8,128)S(1)} %get-tuple-element.65), channel_id=1, source_target_pairs={{0,1},{1,2},{2,3},{4,5},{5,6},{6,7},{8,9},{9,10},{10,11},{12,13},{... | collective-permute-start | bytes 6008 | tf_op jit(solution)/shard_map/ppermute | solution.py:28
  106.2 10.8 %collective-permute-start.5 = (f32[5,10,10,1]{3,2,1,0:T(8,128)S(1)}, f32[5,10,10,1]{3,2,1,0:T(8,128)S(1)}, u32[]{:S(2)}, u32[]{:S(2)}) collective-permute-start(f32[5,10,10,1]{3,2,1,0:T(8,128)S(1)} %get-tuple-element.66), channel_id=1, source_target_pairs={{1,0},{2,1},{3,2},{5,4},{6,5},{7,6},{9,8},{10,9},{11,10},{13,12},{... | collective-permute-start | bytes 6008 | tf_op jit(solution)/shard_map/ppermute | solution.py:29
  160.2 1.3 copy-start.12
  160.3 14.9 %copy-start.10 = (s32[1,1,1,3]{3,2,1,0:T(1,128)S(1)}, s32[1,1,1,3]{3,2,1,0:T(1,128)}, u32[]{:S(2)}) copy-start(s32[1,1,1,3]{3,2,1,0:T(1,128)} %param.20) | copy-start | bytes 40
  161.9 5.6 collective-permute-start.6
  166.2 4.5 collective-permute-start.7
  170.7 5.1 collective-permute-start.8
  173.8 4.5 collective-permute-start.9
  175.8 47.6 %copy-start.9 = (f32[8]{0:T(128)S(1)}, f32[8]{0:T(128)}, u32[]{:S(2)}) copy-start(f32[8]{0:T(128)} %constant.59.clone) | copy-start | bytes 100
  178.6 7.3 %collective-permute-start.10 = (f32[3,10,10,1]{3,0,2,1:T(4,128)S(1)}, f32[3,10,10,1]{3,0,2,1:T(4,128)S(1)}, u32[]{:S(2)}, u32[]{:S(2)}) collective-permute-start(f32[3,10,10,1]{3,0,2,1:T(4,128)S(1)} %get-tuple-element.88), channel_id=1, source_target_pairs={{0,1},{1,2},{2,3},{4,5},{5,6},{6,7},{8,9},{9,10},{10,11},{12,13},{... | collective-permute-start | bytes 3608 | tf_op jit(solution)/shard_map/ppermute | solution.py:28
  183.2 8.6 %collective-permute-start.11 = (f32[3,10,10,1]{3,0,2,1:T(4,128)S(1)}, f32[3,10,10,1]{3,0,2,1:T(4,128)S(1)}, u32[]{:S(2)}, u32[]{:S(2)}) collective-permute-start(f32[3,10,10,1]{3,0,2,1:T(4,128)S(1)} %get-tuple-element.89), channel_id=1, source_target_pairs={{1,0},{2,1},{3,2},{5,4},{6,5},{7,6},{9,8},{10,9},{11,10},{13,12},{... | collective-permute-start | bytes 3608 | tf_op jit(solution)/shard_map/ppermute | solution.py:29
  192.1 5.3 collective-permute-start.12
  196.1 6.0 collective-permute-start.13
  202.1 5.1 collective-permute-start.14
  205.3 4.5 collective-permute-start.15
  210.0 12.2 %collective-permute-start.16 = (f32[3,10,10,1]{3,0,2,1:T(4,128)S(1)}, f32[3,10,10,1]{3,0,2,1:T(4,128)S(1)}, u32[]{:S(2)}, u32[]{:S(2)}) collective-permute-start(f32[3,10,10,1]{3,0,2,1:T(4,128)S(1)} %get-tuple-element.86), channel_id=1, source_target_pairs={{0,1},{1,2},{2,3},{4,5},{5,6},{6,7},{8,9},{9,10},{10,11},{12,13},{... | collective-permute-start | bytes 3608 | tf_op jit(solution)/shard_map/ppermute | solution.py:28
  214.4 8.6 %collective-permute-start.17 = (f32[3,10,10,1]{3,0,2,1:T(4,128)S(1)}, f32[3,10,10,1]{3,0,2,1:T(4,128)S(1)}, u32[]{:S(2)}, u32[]{:S(2)}) collective-permute-start(f32[3,10,10,1]{3,0,2,1:T(4,128)S(1)} %get-tuple-element.87), channel_id=1, source_target_pairs={{1,0},{2,1},{3,2},{5,4},{6,5},{7,6},{9,8},{10,9},{11,10},{13,12},{... | collective-permute-start | bytes 3608 | tf_op jit(solution)/shard_map/ppermute | solution.py:29
  223.3 25.0 %copy-start.4 = (f32[3,8,8,128]{3,2,1,0:T(8,128)}, f32[3,8,8,128]{3,2,1,0:T(8,128)S(1)}, u32[]{:S(2)}) copy-start(f32[3,8,8,128]{3,2,1,0:T(8,128)S(1)} %copy.242) | copy-start | bytes 294916
  325.2 278.5 %copy-start.1 = (f32[3,5,5]{2,0,1:T(4,128)S(1)}, f32[3,5,5]{2,0,1:T(4,128)}, u32[]{:S(2)}) copy-start(f32[3,5,5]{2,0,1:T(4,128)} %param.15) | copy-start | bytes 904
Sparse Core Ops, SparseCore 0:
  325.3 276.6 all-reduce.2
where the time goes:
time: 613 us; the launch traced here: 611 us
  waiting for transfers between devices  303 us (49%)
  local copies, waits for them, and re-layouts  205 us (33%)
  starting transfers between devices  52.8 us (9%)
  other arithmetic  27.1 us (4%)
  between operations  20.9 us (3%)
    unnamed x2, waiting for transfers between devices  277 us
    slice x37, local copies, waits for them, and re-layouts, flux_sweep(): jacobian[direction, source].astype(jnp.float32)  60.5 us
    reshape x1, local copies, waits for them, and re-layouts, local(): full.reshape(boxes, 3, groups, share).transpose(0, 2, 1, 3)  60.3 us
    ppermute x9, starting transfers between devices, padded_2(): before = lax.ppermute(last, axis, up)  38.6 us
    mul x38, local copies, waits for them, and re-layouts, flux_sweep(): jacobian[direction, source].astype(jnp.float32)  35.1 us
    add x1, other arithmetic, flux_sweep(): total + jacobian[direction, source].astype(jnp.float32) * shifted[directi...  25.7 us
    ppermute x9, waiting for transfers between devices, padded_2(): after = lax.ppermute(first, axis, down)  25.1 us
    broadcast_in_dim x1, local copies, waits for them, and re-layouts, local(): full = jnp.zeros((boxes, 3, LA, LB, LC), jnp.float32)  23.8 us
  transfers between devices with their start and end apart: 19, of which 9 were waited for; matrix products, arithmetic and copies ran while one was open for 13% of the time, Pallas kernels for 0%

commit v1 on v0

v1 whole, which is shorter than its diff:
```python
import functools
import math

import jax
import jax.numpy as jnp
import numpy as np
from jax import lax
from jax.experimental import pallas as pl
from jax.experimental.pallas import tpu as pltpu
from jax.sharding import PartitionSpec as P

F32 = jnp.float32
HIGHEST = lax.Precision.HIGHEST
CN = ("chord", "normal")
CX, CY, CZ = 8, 8, 128
LA, LB, LC = 96, 32, 16
ROWS = LA // 16
SLOT = 32
KEEP = 24


def bernstein(count, cells):
    degree = count - 1
    u = (np.arange(cells) + 0.5) / cells
    return np.stack([math.comb(degree, a) * u**a * (1 - u) ** (degree - a) for a in range(count)])


def tables():
    bx, by, bz = bernstein(8, CX), bernstein(8, CY), bernstein(8, CZ)
    along_z = np.zeros((CZ, 8, 16))
    along_z[:, :, :8] = bz.T[:, None, :]
    along_y = np.repeat(by.T, 16, axis=1)
    along_x = np.zeros((3, 8, 3, CX, CY))
    for r in range(3):
        along_x[r, :, r] = 8.0 * bx[:, :, None]
    return (
        along_z.reshape(CZ, 128).astype(np.float32),
        along_y.astype(np.float32),
        along_x.reshape(24, 192).astype(np.float32),
    )


def iotas():
    lane = lax.broadcasted_iota(jnp.int32, (8, 128), 1)
    row = lax.broadcasted_iota(jnp.int32, (8, 128), 0)
    return lane, row


def places():
    c = lax.axis_index("chord")
    n = lax.axis_index("normal")
    before = (jnp.maximum(c - 1, 0) * 4 + n, c * 4 + jnp.maximum(n - 1, 0))
    after = (jnp.minimum(c + 1, 3) * 4 + n, c * 4 + jnp.minimum(n + 1, 3))
    return c, n, before, after


def pack(tile_of, fields, first_ref, last_ref, slots_ref):
    lane, _ = iotas()
    _, _, before, after = places()
    low = jnp.zeros((8, 128), F32)
    high = jnp.zeros((8, 128), F32)
    for v in range(fields):
        for x in range(CX):
            tile = tile_of(v, x)
            k = v * CX + x
            if x == 0:
                first_ref[v] = tile
            if x == CX - 1:
                last_ref[v] = tile
            slots_ref[before[0], k : k + 1, :] = tile[0:1, :]
            slots_ref[after[0], k : k + 1, :] = tile[7:8, :]
            low = jnp.where(lane == k, pltpu.roll(tile, k, 1) if k else tile, low)
            high = jnp.where(lane == k, pltpu.roll(tile, k + 1, 1), high)
    slots_ref[before[1], 0:8, :] = low
    slots_ref[after[1], 0:8, :] = high


def unpack(fields, slots_ref, rows_ref):
    c, n, before, after = places()
    count = fields * CX
    rows_ref[0] = jnp.where(c > 0, slots_ref[before[0], 0:count, :], 0.0)
    rows_ref[1] = jnp.where(c < 3, slots_ref[after[0], 0:count, :], 0.0)
    low = jnp.where(n > 0, slots_ref[before[1], 0:8, :], 0.0)
    high = jnp.where(n < 3, slots_ref[after[1], 0:8, :], 0.0)
    return low, high


def neighbours(tile_of, v, x, xlo_ref, xhi_ref, rows_ref, low, high):
    lane, row = iotas()
    k = v * CX + x
    tile = tile_of(v, x)
    west = xlo_ref[v] if x == 0 else tile_of(v, x - 1)
    east = xhi_ref[v] if x == CX - 1 else tile_of(v, x + 1)
    south = jnp.where(row == 0, rows_ref[0, k : k + 1, :], pltpu.roll(tile, 1, 0))
    north = jnp.where(row == 7, rows_ref[1, k : k + 1, :], pltpu.roll(tile, 7, 0))
    down = jnp.where(lane == 0, pltpu.roll(low, (128 - k) % 128, 1) if k else low, pltpu.roll(tile, 1, 1))
    up = jnp.where(lane == 127, pltpu.roll(high, 127 - k, 1), pltpu.roll(tile, 127, 1))
    return [tile, west, east, south, north, down, up]


def edges_kernel(adjoint_ref, first_ref, last_ref, slots_ref):
    pack(lambda v, x: adjoint_ref[v, x], 5, first_ref, last_ref, slots_ref)


def flux_kernel(
    wall_ref, map_ref, adjoint_ref, jacobian_ref, face_ref, stiff_ref, xlo_ref, xhi_ref, slots_ref,
    out_ref, first_ref, last_ref, send_ref, rows_ref,
):
    lane, row = iotas()
    n = lax.axis_index("normal")
    low, high = unpack(5, slots_ref, rows_ref)
    tile_of = lambda v, x: adjoint_ref[v, x]
    on_wall = (lane == 0) & (n == 0)
    for x in range(CX):
        total = [jnp.zeros((8, 128), F32) for _ in range(5)]
        faces = jnp.broadcast_to(face_ref[x : x + 1, :], (8, 8))
        square = lax.broadcasted_iota(jnp.int32, (8, 8), 0) == lax.broadcasted_iota(jnp.int32, (8, 8), 1)
        face = jnp.sum(jnp.where(square, faces.astype(F32), 0.0), axis=1, keepdims=True)
        kind = [on_wall & (jnp.broadcast_to(face, (8, 128)) == float(t)) for t in range(3)]
        for p in range(5):
            views = neighbours(tile_of, p, x, xlo_ref, xhi_ref, rows_ref, low, high)
            for e in range(7):
                for q in range(5):
                    total[q] = total[q] + jacobian_ref[e, p, q, x].astype(F32) * views[e]
            for t in range(3):
                part = jnp.where(kind[t], views[0], 0.0)
                for q in range(5):
                    total[q] = total[q] + wall_ref[t, p * 5 + q] * part
        diagonal = stiff_ref[0, x]
        for e in range(1, 7):
            diagonal = diagonal + stiff_ref[e, x]
        inverse = 1.0 / diagonal
        for r in range(3):
            sens = map_ref[r, 0] * total[0]
            for q in range(1, 5):
                sens = sens + map_ref[r, q] * total[q]
            out_ref[r, x] = sens * inverse
    pack(lambda v, x: out_ref[v, x], 3, first_ref, last_ref, send_ref)


def sweep(now_ref, start_ref, stiff_ref, xlo_ref, xhi_ref, slots_ref, rows_ref, store):
    low, high = unpack(3, slots_ref, rows_ref)
    tile_of = lambda v, x: now_ref[v, x]
    for x in range(CX):
        diagonal = stiff_ref[0, x]
        for e in range(1, 7):
            diagonal = diagonal + stiff_ref[e, x]
        inverse = 1.0 / diagonal
        for v in range(3):
            views = neighbours(tile_of, v, x, xlo_ref, xhi_ref, rows_ref, low, high)
            total = stiff_ref[1, x] * views[1]
            for e in range(2, 7):
                total = total + stiff_ref[e, x] * views[e]
            store(v, x, start_ref[v, x] + total * inverse)


def middle_kernel(
    start_ref, stiff_ref, xlo_ref, xhi_ref, slots_ref, out_ref, first_ref, last_ref, send_ref, rows_ref
):
    def store(v, x, tile):
        out_ref[v, x] = tile

    sweep(start_ref, start_ref, stiff_ref, xlo_ref, xhi_ref, slots_ref, rows_ref, store)
    pack(lambda v, x: out_ref[v, x], 3, first_ref, last_ref, send_ref)


def window_kernel(
    box_ref, corner_ref, now_ref, start_ref, stiff_ref, xlo_ref, xhi_ref, slots_ref,
    bz_ref, by_ref, bx_ref, out_ref, send_ref, rows_ref, flat_ref,
):
    def store(v, x, tile):
        out_ref[v, x] = tile
        base = (v * CX + x) * CY
        flat_ref[base : base + CY, :] = tile

    sweep(now_ref, start_ref, stiff_ref, xlo_ref, xhi_ref, slots_ref, rows_ref, store)
    inner = jnp.dot(flat_ref[...], bz_ref[...], precision=HIGHEST, preferred_element_type=F32)
    inner = inner * jnp.concatenate([by_ref[...]] * 24, axis=0)
    window = jnp.dot(bx_ref[...], inner, precision=HIGHEST, preferred_element_type=F32)
    lane, row = iotas()
    box = box_ref[0]
    oa, ob, oc = corner_ref[0], corner_ref[1], corner_ref[2]
    shift = oc + 16 * lax.rem(ob, 8)
    window = pltpu.roll(window, shift, 1)
    block = lax.div(ob, 8) + jnp.where(lane < shift, 1, 0)
    for s in range(16):
        where = jnp.where(box == s, block, -1)
        send_ref[s, 0:24, :] = window
        send_ref[s, 24:32, :] = jnp.where(row == 0, where, oa).astype(F32)


def place_kernel(got_ref, send_ref, wide_ref):
    lane, _ = iotas()
    target = jnp.zeros((8, 128), F32)
    for w in range(16):
        where = jnp.broadcast_to(got_ref[w, 24:25, :], (8, 128))
        start = jnp.broadcast_to(got_ref[w, 25:26, :], (8, 128))
        target = jnp.where(lane // 8 == w, start, target)
        for r in range(3):
            tile = got_ref[w, r * 8 : r * 8 + 8, :]
            for block in range(4):
                wide_ref[r, w * 8 : w * 8 + 8, block * 128 : block * 128 + 128] = jnp.where(
                    where == float(block), tile, 0.0
                )
    target = target + lax.rem(lane, 8).astype(F32)
    line = lax.broadcasted_iota(jnp.int32, (128, 128), 0)
    point = (line // 8) * ROWS + lax.rem(line, 8)
    point = jnp.where(lax.rem(line, 8) < ROWS, point, -1).astype(F32)
    pick = jnp.where(point == jnp.concatenate([target] * 16, axis=0), 1.0, 0.0).astype(F32)
    for r in range(3):
        placed = jnp.dot(pick, wide_ref[r], precision=HIGHEST, preferred_element_type=F32)
        for j in range(16):
            for block in range(4):
                base = (r * 4 + block) * ROWS
                send_ref[j, base : base + ROWS, :] = placed[
                    j * 8 : j * 8 + ROWS, block * 128 : block * 128 + 128
                ]


def sum_kernel(got_ref, out_ref, total_ref):
    total = got_ref[0]
    for j in range(1, 16):
        total = total + got_ref[j]
    total_ref[...] = total
    for r in range(3):
        for block in range(4):
            for a in range(ROWS):
                base = a * 512 + block * 128
                at = (r * 4 + block) * ROWS + a
                out_ref[0, r : r + 1, base : base + 128] = total_ref[at : at + 1, :]


VMEM = pl.BlockSpec(memory_space=pltpu.VMEM)
SMEM = pl.BlockSpec(memory_space=pltpu.SMEM)


def shape(*dims):
    return jax.ShapeDtypeStruct(dims, F32)


def call(body, outs, ins, scratch=(), scalars=0, limit=24, name=None):
    return pl.pallas_call(
        body,
        out_shape=outs,
        in_specs=[SMEM] * scalars + [VMEM] * (len(ins) - scalars),
        out_specs=jax.tree.map(lambda _: VMEM, outs),
        scratch_shapes=[pltpu.VMEM(dims, F32) for dims in scratch],
        compiler_params=pltpu.CompilerParams(vmem_limit_bytes=limit << 20),
        name=name,
    )(*ins)


def swap(first, last, slots):
    count = lax.axis_size("span")
    up = [(i, i + 1) for i in range(count - 1)]
    down = [(j, i) for i, j in up]
    got = lax.all_to_all(slots, CN, 0, 0, tiled=True)
    before = lax.ppermute(last, "span", up)
    after = lax.ppermute(first, "span", down)
    return before, after, got


def local(adjoint, jacobian, wall_table, face_type, mesh_map, stiffness, box_map, offsets):
    ends = lambda v, rows: (shape(v, 8, 128), shape(v, 8, 128), shape(16, rows, 128))
    block = shape(3, CX, CY, CZ)
    halo = swap(*call(edges_kernel, ends(5, 40), (adjoint,), name="edges"))
    start, *out = call(
        flux_kernel,
        (block, *ends(3, KEEP)),
        (wall_table.reshape(3, 25), mesh_map, adjoint, jacobian, face_type, stiffness, *halo),
        scratch=((2, 40, 128),),
        scalars=2,
        name="flux",
    )
    halo = swap(*out)
    middle, *out = call(
        middle_kernel, (block, *ends(3, KEEP)), (start, stiffness, *halo), scratch=((2, 24, 128),), name="middle"
    )
    halo = swap(*out)
    bz, by, bx = tables()
    final, windows = call(
        window_kernel,
        (block, shape(16, SLOT, 128)),
        (box_map.reshape(1), offsets.reshape(3), middle, start, stiffness, *halo, bz, by, bx),
        scratch=((2, 24, 128), (192, 128)),
        scalars=2,
        name="window",
    )
    got = lax.all_to_all(windows, "span", 0, 0, tiled=True)
    chunks = call(place_kernel, shape(16, 72, 128), (got,), scratch=((3, 128, 512),), name="place")
    got = lax.all_to_all(chunks, CN, 0, 0, tiled=True)
    grad = call(sum_kernel, shape(1, 3, 3072), (got,), scratch=((72, 128),), name="sums")
    return final, grad


def solution(mesh):
    placed = (
        P(None, "span", "chord", "normal"),
        P(None, None, None, "span", "chord", "normal"),
        P(),
        P("span", "chord"),
        P(),
        P(None, "span", "chord", "normal"),
        P("span", "chord", "normal"),
        P("span", "chord", "normal", None),
    )
    return jax.shard_map(
        local,
        mesh=mesh,
        in_specs=placed,
        out_specs=(P(None, "span", "chord", "normal"), P("span", None, ("chord", "normal"))),
        check_vma=False,
    )
```

time: 613 us -> 103 us (0.17)
  waiting for transfers between devices: 303 us -> 11.1 us
  local copies, waits for them, and re-layouts: 205 us -> 7.45 us
  blocking collectives: 0 us -> 35.7 us
  other arithmetic: 27.1 us -> 0 us
  between operations: 20.9 us -> 1.41 us
  starting transfers between devices: 52.8 us -> 40 us
  Pallas kernels: 0 us -> 6.84 us
    unnamed x2 -> x0, waiting for transfers between devices: 277 us -> none
    slice x45 -> x0, local copies, waits for them, and re-layouts: 63.1 us -> none  [the longest x37 60.5 us: flux_sweep(): jacobian[direction, source].astype(jnp.float32)]
    reshape x1, local copies, waits for them, and re-layouts: 60.3 us -> 0.08 us  [local(): wall_table.reshape(3, 25)]
    ppermute x18 -> x6, starting transfers between devices: 52.7 us -> 15.8 us  [the longest x3 11.9 us: swap(): before = lax.ppermute(last, 'span', up)]
    all_to_all x0 -> x2, blocking collectives: none -> 35.7 us  [the longest x1 22.8 us: local(): got = lax.all_to_all(chunks, CN, 0, 0, tiled=True)]
    mul x38 -> x0, local copies, waits for them, and re-layouts: 35.1 us -> none  [flux_sweep(): jacobian[direction, source].astype(jnp.float32)]
    add x3 -> x0, other arithmetic: 26.4 us -> none  [the longest x1 25.7 us: flux_sweep(): total + jacobian[direction, source].astype(jnp.float32) * shifted[directi...]
    all_to_all x0 -> x3, starting transfers between devices: none -> 24.2 us  [swap(): got = lax.all_to_all(slots, CN, 0, 0, tiled=True)]
  transfers between devices with their start and end apart: 19 -> 9, of which waited for: 9 -> 4; matrix products, arithmetic and copies ran while one was open for 13% -> 1% of each run, Pallas kernels for 0% -> 0%
where the time goes in v1:
time: 103 us; the launch traced here: 102 us
  starting transfers between devices  40 us (39%)
  blocking collectives  35.7 us (35%)
  waiting for transfers between devices  11.1 us (11%)
  local copies, waits for them, and re-layouts  7.45 us (7%)
  Pallas kernels  6.84 us (7%)
  between operations  1.41 us (1%)
    all_to_all x3, starting transfers between devices, swap(): got = lax.all_to_all(slots, CN, 0, 0, tiled=True)  24.2 us
    all_to_all x1, blocking collectives, local(): got = lax.all_to_all(chunks, CN, 0, 0, tiled=True)  22.8 us
    all_to_all x1, blocking collectives, local(): got = lax.all_to_all(windows, 'span', 0, 0, tiled=True)  12.9 us
    ppermute x3, starting transfers between devices, swap(): before = lax.ppermute(last, 'span', up)  11.9 us
    ppermute x3, waiting for transfers between devices, swap(): after = lax.ppermute(first, 'span', down)  10.1 us
    unnamed x24, local copies, waits for them, and re-layouts  7.36 us
    pallas_call x6, Pallas kernels, call(): pl.pallas_call(body, out_shape=outs, in_specs=[SMEM] * scalars + [VMEM] *...  6.84 us
    ppermute x3, starting transfers between devices, swap(): after = lax.ppermute(first, 'span', down)  3.88 us
  transfers between devices with their start and end apart: 9, of which 4 were waited for; matrix products, arithmetic and copies ran while one was open for 1% of the time, Pallas kernels for 0%

profile of v1, /device:TPU:1, one launch (start us, length us, event | category | flops | bytes accessed | tf_op | source)
XLA Modules:
  0.0 102.5 jit_solution(18241066429277381516)
XLA Ops:
  0.6 0.0 copy-start.2
  0.6 0.0 copy-start.3
  0.7 0.9 copy-done.3
  1.6 0.9 edges.1
  2.5 0.0 copy-start.5
  2.5 0.0 copy-start.6
  2.5 0.0 copy-start.8
  2.5 0.0 copy-start.10
  2.5 8.6 %all-to-all-start = ((f32[16,40,128]{2,1,0:T(8,128)}), f32[16,40,128]{2,1,0:T(8,128)S(1)}, u32[]{:S(2)}, u32[]{:S(2)}) async-start(f32[16,40,128]{2,1,0:T(8,128)} %get-tuple-element.17), calls=%async_computation | async-start | bytes 655360 | tf_op jit(solution)/shard_map/all_to_all | solution.py:257
  11.1 3.5 %collective-permute-start = (f32[5,8,128]{2,1,0:T(8,128)S(1)}, f32[5,8,128]{2,1,0:T(8,128)S(1)}, u32[]{:S(2)}, u32[]{:S(2)}) collective-permute-start(f32[5,8,128]{2,1,0:T(8,128)S(1)} %get-tuple-element.15), channel_id=1, source_target_pairs={{0,16},{16,32},{32,48},{48,64},{64,80},{80,96},{96,112},{112,128},... | collective-permute-start | bytes 61448 | tf_op jit(solution)/shard_map/ppermute | solution.py:258
  14.6 1.3 %collective-permute-start.1 = (f32[5,8,128]{2,1,0:T(8,128)S(1)}, f32[5,8,128]{2,1,0:T(8,128)S(1)}, u32[]{:S(2)}, u32[]{:S(2)}) collective-permute-start(f32[5,8,128]{2,1,0:T(8,128)S(1)} %get-tuple-element.16), channel_id=1, source_target_pairs={{16,0},{32,16},{48,32},{64,48},{80,64},{96,80},{112,96},{128,112},... | collective-permute-start | bytes 61448 | tf_op jit(solution)/shard_map/ppermute | solution.py:259
  15.9 0.7 copy.15
  16.6 0.1 reshape.15.wall_ref
  16.7 0.0 collective-permute-done.xlo_ref
  16.7 2.9 %collective-permute-done.1.xhi_ref = f32[5,8,128]{2,1,0:T(8,128)S(1)} collective-permute-done((f32[5,8,128]{2,1,0:T(8,128)S(1)}, f32[5,8,128]{2,1,0:T(8,128)S(1)}, u32[]{:S(2)}, u32[]{:S(2)}) %collective-permute-start.1) | collective-permute-done | bytes 20512 | tf_op jit(solution)/shard_map/ppermute | solution.py:259
  19.6 0.9 all-to-all-done.slots_ref
  20.6 0.0 copy-start
  20.6 1.8 %copy-done = bf16[7,5,5,8,8,128]{5,4,3,2,1,0:T(8,128)(2,1)S(1)} copy-done((bf16[7,5,5,8,8,128]{5,4,3,2,1,0:T(8,128)(2,1)S(1)}, bf16[7,5,5,8,8,128]{5,4,3,2,1,0:T(8,128)(2,1)}, u32[]{:S(2)}) %copy-start) | copy-done | bytes 2867224
  22.4 0.0 copy-start.1
  22.4 0.9 copy-done.1
  23.3 0.9 copy-done.4
  24.2 0.7 copy-done.7
  24.9 0.7 copy-done.9
  25.6 2.4 %flux.1 = (f32[3,8,8,128]{3,2,1,0:T(8,128)S(1)}, f32[3,8,128]{2,1,0:T(8,128)S(1)}, f32[3,8,128]{2,1,0:T(8,128)S(1)}, f32[16,24,128]{2,1,0:T(8,128)}) custom-call(f32[3,25]{1,0:T(4,128)S(1)} %reshape.15.wall_ref, f32[3,5]{1,0:T(4,128)S(1)} %copy-done.9, f32[5,8,8,128]{3,2,1,0:T(8,128)S(1)} %copy-done.4, bf16[7,5,5,8,8,128]{5,4,3,2,1,0:T(8,128)(2,1)S(1)} %copy-done, ...), custom_call_target="tpu_custom_call" | custom-call | tf_op jit(solution)/shard_map/flux/pallas_call | solution.py:242
  28.0 7.2 %all-to-all-start.1 = ((f32[16,24,128]{2,1,0:T(8,128)}), f32[16,24,128]{2,1,0:T(8,128)S(1)}, u32[]{:S(2)}, u32[]{:S(2)}) async-start(f32[16,24,128]{2,1,0:T(8,128)} %get-tuple-element.21), calls=%async_computation.1 | async-start | bytes 393216 | tf_op jit(solution)/shard_map/all_to_all | solution.py:257
  35.3 3.5 %collective-permute-start.2 = (f32[3,8,128]{2,1,0:T(8,128)S(1)}, f32[3,8,128]{2,1,0:T(8,128)S(1)}, u32[]{:S(2)}, u32[]{:S(2)}) collective-permute-start(f32[3,8,128]{2,1,0:T(8,128)S(1)} %get-tuple-element.19), channel_id=1, source_target_pairs={{0,16},{16,32},{32,48},{48,64},{64,80},{80,96},{96,112},{112,128},... | collective-permute-start | bytes 36872 | tf_op jit(solution)/shard_map/ppermute | solution.py:258
  38.8 1.3 %collective-permute-start.3 = (f32[3,8,128]{2,1,0:T(8,128)S(1)}, f32[3,8,128]{2,1,0:T(8,128)S(1)}, u32[]{:S(2)}, u32[]{:S(2)}) collective-permute-start(f32[3,8,128]{2,1,0:T(8,128)S(1)} %get-tuple-element.20), channel_id=1, source_target_pairs={{16,0},{32,16},{48,32},{64,48},{80,64},{96,80},{112,96},{128,112},... | collective-permute-start | bytes 36872 | tf_op jit(solution)/shard_map/ppermute | solution.py:259
  40.1 0.0 collective-permute-done.2.xlo_ref
  40.1 4.4 %collective-permute-done.3.xhi_ref = f32[3,8,128]{2,1,0:T(8,128)S(1)} collective-permute-done((f32[3,8,128]{2,1,0:T(8,128)S(1)}, f32[3,8,128]{2,1,0:T(8,128)S(1)}, u32[]{:S(2)}, u32[]{:S(2)}) %collective-permute-start.3) | collective-permute-done | bytes 12320 | tf_op jit(solution)/shard_map/ppermute | solution.py:259
  44.5 0.0 all-to-all-done.1.slots_ref
  44.6 0.0 copy-done.2
  44.6 0.9 middle.1
  45.5 8.4 %all-to-all-start.2 = ((f32[16,24,128]{2,1,0:T(8,128)}), f32[16,24,128]{2,1,0:T(8,128)S(1)}, u32[]{:S(2)}, u32[]{:S(2)}) async-start(f32[16,24,128]{2,1,0:T(8,128)} %get-tuple-element.25), calls=%async_computation.2 | async-start | bytes 393216 | tf_op jit(solution)/shard_map/all_to_all | solution.py:257
  53.9 4.8 %collective-permute-start.4 = (f32[3,8,128]{2,1,0:T(8,128)S(1)}, f32[3,8,128]{2,1,0:T(8,128)S(1)}, u32[]{:S(2)}, u32[]{:S(2)}) collective-permute-start(f32[3,8,128]{2,1,0:T(8,128)S(1)} %get-tuple-element.23), channel_id=1, source_target_pairs={{0,16},{16,32},{32,48},{48,64},{64,80},{80,96},{96,112},{112,128},... | collective-permute-start | bytes 36872 | tf_op jit(solution)/shard_map/ppermute | solution.py:258
  58.7 1.3 %collective-permute-start.5 = (f32[3,8,128]{2,1,0:T(8,128)S(1)}, f32[3,8,128]{2,1,0:T(8,128)S(1)}, u32[]{:S(2)}, u32[]{:S(2)}) collective-permute-start(f32[3,8,128]{2,1,0:T(8,128)S(1)} %get-tuple-element.24), channel_id=1, source_target_pairs={{16,0},{32,16},{48,32},{64,48},{80,64},{96,80},{112,96},{128,112},... | collective-permute-start | bytes 36872 | tf_op jit(solution)/shard_map/ppermute | solution.py:259
  60.7 0.0 collective-permute-done.4.xlo_ref
  60.7 2.8 %collective-permute-done.5.xhi_ref = f32[3,8,128]{2,1,0:T(8,128)S(1)} collective-permute-done((f32[3,8,128]{2,1,0:T(8,128)S(1)}, f32[3,8,128]{2,1,0:T(8,128)S(1)}, u32[]{:S(2)}, u32[]{:S(2)}) %collective-permute-start.5) | collective-permute-done | bytes 12320 | tf_op jit(solution)/shard_map/ppermute | solution.py:259
  63.4 0.0 all-to-all-done.2.slots_ref
  63.4 0.0 copy-done.5
  63.5 0.0 copy-done.6
  63.5 0.0 copy-done.8
  63.5 0.0 copy-done.10
  63.5 1.7 %window.1 = (f32[3,8,8,128]{3,2,1,0:T(8,128)}, f32[16,32,128]{2,1,0:T(8,128)S(1)}) custom-call(s32[1]{0:T(128)} %bitcast.2.box_ref, s32[3]{0:T(128)S(1)} %bitcast.3, f32[3,8,8,128]{3,2,1,0:T(8,128)S(1)} %get-tuple-element.22.now_ref, f32[3,8,8,128]{3,2,1,0:T(8,128)S(1)} %get-tuple-element.18.start_ref, f32[7,8,8,128]{3,2,1,0:T(8,128)S(1)} %copy-done.2, ...), custom_call_target="tpu_custom_call" | custom-call | tf_op jit(solution)/shard_map/window/pallas_call | solution.py:242
  65.2 12.9 %all_to_all.25.got_ref = f32[16,32,128]{2,1,0:T(8,128)S(1)} all-to-all(f32[16,32,128]{2,1,0:T(8,128)S(1)} %get-tuple-element.27), channel_id=1, replica_groups=mesh['span'=16,'chord'=4,'normal'=4] {'span'}, dimensions={0} | all-to-all | bytes 524288 | tf_op jit(solution)/shard_map/all_to_all | solution.py:289
  78.1 0.8 place.1
  79.0 22.8 %all_to_all.26.got_ref = f32[16,72,128]{2,1,0:T(8,128)S(1)} all-to-all(f32[16,72,128]{2,1,0:T(8,128)S(1)} %place.1), channel_id=1, replica_groups=mesh['span'=16,'chord'=4,'normal'=4] {'chord','normal'}, dimensions={0} | all-to-all | bytes 1179648 | tf_op jit(solution)/shard_map/all_to_all | solution.py:291
  101.7 0.1 sums.1
  101.8 0.7 copy.16
  (3 shorter events, 0.0 us)
Async XLA Ops:
  0.6 43.9 %copy-start.2 = (f32[7,8,8,128]{3,2,1,0:T(8,128)S(1)}, f32[7,8,8,128]{3,2,1,0:T(8,128)}, u32[]{:S(2)}) copy-start(f32[7,8,8,128]{3,2,1,0:T(8,128)} %stiff_ref.5) | copy-start | bytes 688132
  0.6 1.0 copy-start.3
  2.5 61.0 %copy-start.5 = (f32[128,128]{1,0:T(8,128)S(1)}, f32[128,128]{1,0:T(8,128)}, u32[]{:S(2)}) copy-start(f32[128,128]{1,0:T(8,128)} %constant.6.clone.bz_ref) | copy-start | bytes 196612
  2.5 61.0 %copy-start.6 = (f32[24,192]{1,0:T(8,128)S(1)}, f32[24,192]{1,0:T(8,128)}, u32[]{:S(2)}) copy-start(f32[24,192]{1,0:T(8,128)} %constant.8.clone.bx_ref) | copy-start | bytes 55300
  2.5 61.0 %copy-start.8 = (f32[8,128]{1,0:T(8,128)S(1)}, f32[8,128]{1,0:T(8,128)}, u32[]{:S(2)}) copy-start(f32[8,128]{1,0:T(8,128)} %constant.7.clone.by_ref) | copy-start | bytes 12292
  2.5 61.0 %copy-start.10 = (s32[1,1,1,3]{3,2,1,0:T(1,128)S(1)}, s32[1,1,1,3]{3,2,1,0:T(1,128)}, u32[]{:S(2)}) copy-start(s32[1,1,1,3]{3,2,1,0:T(1,128)} %param.18) | copy-start | bytes 40
  2.5 18.1 %all-to-all-start = ((f32[16,40,128]{2,1,0:T(8,128)}), f32[16,40,128]{2,1,0:T(8,128)S(1)}, u32[]{:S(2)}, u32[]{:S(2)}) async-start(f32[16,40,128]{2,1,0:T(8,128)} %get-tuple-element.17), calls=%async_computation | async-start | bytes 655360 | tf_op jit(solution)/shard_map/all_to_all | solution.py:257
  11.1 5.6 %collective-permute-start = (f32[5,8,128]{2,1,0:T(8,128)S(1)}, f32[5,8,128]{2,1,0:T(8,128)S(1)}, u32[]{:S(2)}, u32[]{:S(2)}) collective-permute-start(f32[5,8,128]{2,1,0:T(8,128)S(1)} %get-tuple-element.15), channel_id=1, source_target_pairs={{0,16},{16,32},{32,48},{48,64},{64,80},{80,96},{96,112},{112,128},... | collective-permute-start | bytes 61448 | tf_op jit(solution)/shard_map/ppermute | solution.py:258
  14.6 5.0 %collective-permute-start.1 = (f32[5,8,128]{2,1,0:T(8,128)S(1)}, f32[5,8,128]{2,1,0:T(8,128)S(1)}, u32[]{:S(2)}, u32[]{:S(2)}) collective-permute-start(f32[5,8,128]{2,1,0:T(8,128)S(1)} %get-tuple-element.16), channel_id=1, source_target_pairs={{16,0},{32,16},{48,32},{64,48},{80,64},{96,80},{112,96},{128,112},... | collective-permute-start | bytes 61448 | tf_op jit(solution)/shard_map/ppermute | solution.py:259
  20.6 1.8 %copy-start = (bf16[7,5,5,8,8,128]{5,4,3,2,1,0:T(8,128)(2,1)S(1)}, bf16[7,5,5,8,8,128]{5,4,3,2,1,0:T(8,128)(2,1)}, u32[]{:S(2)}) copy-start(bf16[7,5,5,8,8,128]{5,4,3,2,1,0:T(8,128)(2,1)} %jacobian_ref.1) | copy-start | bytes 8601604
  22.4 0.9 copy-start.1
  23.3 0.9 copy-start.4
  24.2 0.7 copy-start.7
  24.9 0.7 copy-start.9
  28.0 16.5 %all-to-all-start.1 = ((f32[16,24,128]{2,1,0:T(8,128)}), f32[16,24,128]{2,1,0:T(8,128)S(1)}, u32[]{:S(2)}, u32[]{:S(2)}) async-start(f32[16,24,128]{2,1,0:T(8,128)} %get-tuple-element.21), calls=%async_computation.1 | async-start | bytes 393216 | tf_op jit(solution)/shard_map/all_to_all | solution.py:257
  35.3 4.8 %collective-permute-start.2 = (f32[3,8,128]{2,1,0:T(8,128)S(1)}, f32[3,8,128]{2,1,0:T(8,128)S(1)}, u32[]{:S(2)}, u32[]{:S(2)}) collective-permute-start(f32[3,8,128]{2,1,0:T(8,128)S(1)} %get-tuple-element.19), channel_id=1, source_target_pairs={{0,16},{16,32},{32,48},{48,64},{64,80},{80,96},{96,112},{112,128},... | collective-permute-start | bytes 36872 | tf_op jit(solution)/shard_map/ppermute | solution.py:258
  38.8 5.7 %collective-permute-start.3 = (f32[3,8,128]{2,1,0:T(8,128)S(1)}, f32[3,8,128]{2,1,0:T(8,128)S(1)}, u32[]{:S(2)}, u32[]{:S(2)}) collective-permute-start(f32[3,8,128]{2,1,0:T(8,128)S(1)} %get-tuple-element.20), channel_id=1, source_target_pairs={{16,0},{32,16},{48,32},{64,48},{80,64},{96,80},{112,96},{128,112},... | collective-permute-start | bytes 36872 | tf_op jit(solution)/shard_map/ppermute | solution.py:259
  45.5 17.9 %all-to-all-start.2 = ((f32[16,24,128]{2,1,0:T(8,128)}), f32[16,24,128]{2,1,0:T(8,128)S(1)}, u32[]{:S(2)}, u32[]{:S(2)}) async-start(f32[16,24,128]{2,1,0:T(8,128)} %get-tuple-element.25), calls=%async_computation.2 | async-start | bytes 393216 | tf_op jit(solution)/shard_map/all_to_all | solution.py:257
  53.9 6.8 %collective-permute-start.4 = (f32[3,8,128]{2,1,0:T(8,128)S(1)}, f32[3,8,128]{2,1,0:T(8,128)S(1)}, u32[]{:S(2)}, u32[]{:S(2)}) collective-permute-start(f32[3,8,128]{2,1,0:T(8,128)S(1)} %get-tuple-element.23), channel_id=1, source_target_pairs={{0,16},{16,32},{32,48},{48,64},{64,80},{80,96},{96,112},{112,128},... | collective-permute-start | bytes 36872 | tf_op jit(solution)/shard_map/ppermute | solution.py:258
  58.7 4.7 %collective-permute-start.5 = (f32[3,8,128]{2,1,0:T(8,128)S(1)}, f32[3,8,128]{2,1,0:T(8,128)S(1)}, u32[]{:S(2)}, u32[]{:S(2)}) collective-permute-start(f32[3,8,128]{2,1,0:T(8,128)S(1)} %get-tuple-element.24), channel_id=1, source_target_pairs={{16,0},{32,16},{48,32},{64,48},{80,64},{96,80},{112,96},{128,112},... | collective-permute-start | bytes 36872 | tf_op jit(solution)/shard_map/ppermute | solution.py:259
